TPU v7x, 128 devices: a whole 4x4x4 slice. The times are simulated.
128 devices in a mesh: dom: 128 (over x, z, y, core).
Axes of the slice: x: 4, y: 4, z: 4, core: 2. Of those that a mesh axis runs over, the one named last changes fastest.
Arguments:
- features: bfloat16 [262144, 512], P('dom'), may hold values from -6 to 6
- weight: bfloat16 [512, 512], replicated, may hold values from -0.25 to 0.25
- cotangent: bfloat16 [262144, 512], P('dom'), may hold values from -6 to 6
- tile_values: bfloat16 [12288, 128, 128], P('dom'), may hold values from -0.21875 to 0.21875
- tile_rows: int32 [12288], P('dom'), may hold values from 0 to 15
- tile_cols: int32 [12288], P('dom'), may hold values from 0 to 27, as said below
- hub_rows: int32 [512], P('dom'), may hold values from 0 to 2047
- send_rows: int32 [128, 128, 8], P('dom'), may hold values from 0 to 2047
- send_count: int32 [128, 128], P('dom'), may hold values from 1 to 8, as said below
Outputs:
- output: bfloat16 [262144, 512], P('dom')
- grad_features: bfloat16 [262144, 512], P('dom')
- grad_weight: float32 [512, 512], replicated
Inputs may be any that keep to these rules, and one draw needn't show every extreme that they name: `tile_cols`: on every device the first 64 tiles name column blocks below 20 and the other 32 name blocks from 20 on. `send_count`: every source sends 8 rows to at least one device.
All inputs are finite; a program needn't handle non-finite values.
Results may differ from a plain program's by a relative error of at most 0.019.
Values may be sent and summed in bfloat16 or wider, within the bound.
A program may use at most 128 MiB of HBM per device.

v0:
```python
import math
import jax
import jax.numpy as jnp
from jax import lax
from jax.sharding import PartitionSpec as P

LOC_TILES = 64


def one_hot(index, count):
    return (index[:, None] == jnp.arange(count, dtype=jnp.int32)[None, :]).astype(jnp.bfloat16)


def pick_blocks(index, blocks):
    selector = one_hot(index, blocks.shape[0])
    return jnp.einsum("kc,cjf->kjf", selector, blocks, preferred_element_type=jnp.float32).astype(
        blocks.dtype
    )


def add_into(selector, terms):
    upper = terms.astype(jnp.bfloat16)
    lower = (terms - upper.astype(jnp.float32)).astype(jnp.bfloat16)
    first = jnp.einsum("kr,kif->rif", selector, upper, preferred_element_type=jnp.float32)
    return first + jnp.einsum("kr,kif->rif", selector, lower, preferred_element_type=jnp.float32)


def apply_tiles(values, row_idx, col_idx, table_blocks, running):
    tile_count, tile_size = (values.shape[0], values.shape[1])
    group_size = math.gcd(tile_count, 32)
    row_count = running.shape[0]

    def apply_advance(carry, packed):
        vals_group, rows_group, cols_group = packed
        picked = pick_blocks(cols_group, table_blocks)
        products = jnp.einsum(
            "kij,kjf->kif", vals_group, picked, preferred_element_type=jnp.float32
        )
        return (carry + add_into(one_hot(rows_group, row_count), products), None)

    packed = (
        values.reshape(-1, group_size, tile_size, tile_size),
        row_idx.reshape(-1, group_size),
        col_idx.reshape(-1, group_size),
    )
    result, _ = lax.scan(apply_advance, running, packed)
    return result


def spread_tiles(values, row_idx, col_idx, grad_blocks, running):
    tile_count, tile_size = (values.shape[0], values.shape[1])
    group_size = math.gcd(tile_count, 32)
    col_count = running.shape[0]

    def spread_advance(carry, packed):
        vals_group, rows_group, cols_group = packed
        picked = pick_blocks(rows_group, grad_blocks)
        products = jnp.einsum(
            "kij,kif->kjf", vals_group, picked, preferred_element_type=jnp.float32
        )
        return (carry + add_into(one_hot(cols_group, col_count), products), None)

    packed = (
        values.reshape(-1, group_size, tile_size, tile_size),
        row_idx.reshape(-1, group_size),
        col_idx.reshape(-1, group_size),
    )
    result, _ = lax.scan(spread_advance, running, packed)
    return result


def per_device(
    features, weight, cotangent, tile_values, tile_rows, tile_cols, hub_rows, send_rows, send_count
):
    num_dev = lax.axis_size("dom")
    row_count, feat_width = features.shape
    tile_size = tile_values.shape[1]
    row_blocks = row_count // tile_size
    slot_count = send_rows.shape[2]
    split_at = LOC_TILES
    hub_select = one_hot(hub_rows, row_count)
    hub_local = jnp.dot(hub_select, features, preferred_element_type=jnp.float32).astype(
        jnp.bfloat16
    )
    hub_all = lax.all_gather(hub_local, "dom", axis=0, tiled=True)
    targets = send_rows[0]
    counts = send_count[0]
    live_slots = jnp.arange(slot_count, dtype=jnp.int32)[None, :] < counts[:, None]
    target_select = one_hot(targets.reshape(-1), row_count) * live_slots.reshape(-1, 1).astype(
        jnp.bfloat16
    )
    outgoing = (
        jnp.dot(target_select, features, preferred_element_type=jnp.float32)
        .astype(jnp.bfloat16)
        .reshape(num_dev, slot_count, feat_width)
    )
    incoming = lax.all_to_all(outgoing, "dom", split_axis=0, concat_axis=0, tiled=True)
    near_table = jnp.concatenate([features, hub_all], axis=0).reshape(-1, tile_size, feat_width)
    far_table = incoming.reshape(-1, tile_size, feat_width)
    near_blocks = near_table.shape[0]
    empty = jnp.zeros((row_blocks, tile_size, feat_width), jnp.float32)
    summed = apply_tiles(
        tile_values[:split_at], tile_rows[:split_at], tile_cols[:split_at], near_table, empty
    )
    summed = apply_tiles(
        tile_values[split_at:],
        tile_rows[split_at:],
        tile_cols[split_at:] - near_blocks,
        far_table,
        summed,
    )
    aggregated = summed.reshape(row_count, feat_width).astype(jnp.bfloat16)
    pre_act = jnp.dot(aggregated, weight, preferred_element_type=jnp.float32)
    sigmoid_pre = jax.nn.sigmoid(pre_act)
    output = (pre_act * sigmoid_pre).astype(jnp.bfloat16)
    grad_pre = (
        cotangent.astype(jnp.float32) * sigmoid_pre * (1.0 + pre_act * (1.0 - sigmoid_pre))
    ).astype(jnp.bfloat16)
    weight_term = lax.dot_general(
        aggregated, grad_pre, (((0,), (0,)), ((), ())), preferred_element_type=jnp.float32
    )
    weight_term = weight_term * float(row_count * num_dev) ** (-0.5)
    grad_weight = lax.psum(weight_term, "dom")
    grad_agg = lax.dot_general(
        grad_pre, weight, (((1,), (1,)), ((), ())), preferred_element_type=jnp.float32
    ).astype(jnp.bfloat16)
    grad_blocks = grad_agg.reshape(row_blocks, tile_size, feat_width)
    near_grad = spread_tiles(
        tile_values[:split_at],
        tile_rows[:split_at],
        tile_cols[:split_at],
        grad_blocks,
        jnp.zeros((near_blocks, tile_size, feat_width), jnp.float32),
    )
    far_grad = spread_tiles(
        tile_values[split_at:],
        tile_rows[split_at:],
        tile_cols[split_at:] - near_blocks,
        grad_blocks,
        jnp.zeros((far_table.shape[0], tile_size, feat_width), jnp.float32),
    )
    near_flat = near_grad.reshape(-1, feat_width)
    own_grad = near_flat[:row_count]
    hub_grad = near_flat[row_count:]
    far_flat = far_grad.reshape(num_dev, slot_count, feat_width)
    hub_mine = lax.psum_scatter(hub_grad, "dom", scatter_dimension=0, tiled=True)
    returned = lax.all_to_all(
        far_flat.astype(jnp.bfloat16), "dom", split_axis=0, concat_axis=0, tiled=True
    ).astype(far_flat.dtype)
    hub_part = add_into(hub_select, hub_mine[:, None, :])[:, 0, :]
    halo_part = add_into(target_select, returned.reshape(-1, 1, feat_width))[:, 0, :]
    grad_features = own_grad + hub_part + halo_part
    return (output, grad_features.astype(jnp.bfloat16), grad_weight)


def solution(mesh):
    placed = (
        P("dom", None),
        P(),
        P("dom", None),
        P("dom", None, None),
        P("dom"),
        P("dom"),
        P("dom"),
        P("dom", None, None),
        P("dom", None),
    )
    return jax.shard_map(
        per_device,
        mesh=mesh,
        in_specs=placed,
        out_specs=(P("dom", None), P("dom", None), P()),
        check_vma=False,
    )
```

profile of v0, /device:TPU:1, one launch (start us, length us, event | category | flops | bytes accessed | tf_op | source)
XLA Modules:
  0.0 434.4 jit_solution(5442505142722184858)
XLA Ops:
  9.6 4.9 %fusion.69 = bf16[128,8,512]{2,1,0:T(8,128)(2,1)} fusion(bf16[2048,512]{1,0:T(8,128)(2,1)} %param.13, s32[1024]{0:T(1024)S(1)} %eq.165, bf16[1024]{0:T(1024)(128)(2,1)S(1)} %reshape.143), kind=kOutput, calls=%fused_computation.85 | convolution fusion | flops 2152202240 | bytes 3151872 | tf_op jit(solution)/shard_map/dot_general | solution.py:93
  14.5 12.0 %all-to-all-start = ((bf16[128,8,512]{2,1,0:T(8,128)(2,1)}), bf16[128,8,512]{2,1,0:T(8,128)(2,1)}, u32[]{:S(2)}, u32[]{:S(2)}) async-start(bf16[128,8,512]{2,1,0:T(8,128)(2,1)} %fusion.69), calls=%async_computation | async-start | bytes 2097152 | tf_op jit(solution)/shard_map/all_to_all | solution.py:97
  27.1 45.4 %all-gather = bf16[128,4,512]{2,1,0:T(4,128)(2,1)} all-gather(bf16[1,4,512]{2,1,0:T(4,128)(2,1)S(1)} %fusion.72), channel_id=1, replica_groups=mesh['dom'=128] {'dom'}, dimensions={0}, use_global_device_ids=true | all-gather | bytes 528384 | tf_op jit(solution)/shard_map/all_gather | solution.py:85
  73.8 3.1 copy.67
  77.0 42.9 %while.6 = (s32[]{:T(128)}, f32[16,128,512]{2,0,1:T(8,128)}, s32[2,32]{1,0:T(2,128)S(1)}, bf16[2,32,128,128]{3,2,1,0:T(8,128)(2,1)S(1)}, s32[2,32]{1,0:T(2,128)S...) while((s32[]{:T(128)}, f32[16,128,512]{2,0,1:T(8,128)}, s32[2,32]{1,0:T(2,128)S(1)}, ...), condition=%wide.region_1.2_spmd.clone, body=%wide.region_0.1_spmd.clone.sunk | while | flops 768607872 | bytes 45614052 | solution.py:46
  77.0 3.2 convolution_convert_fusion.8
  80.2 4.3 subtract_convert_fusion.8
  84.4 4.8 %fusion.142 = f32[16,128,512]{2,0,1:T(8,128)} fusion(bf16[32,128,512]{2,1,0:T(8,128)(2,1)S(1)} %get-tuple-element.300, s32[32]{0:T(128)S(1)} %get-tuple-element.301), kind=kOutput, calls=%fused_computation.1.clone.1 | convolution fusion | flops 67109376 | bytes 8388736 | tf_op jit(solution)/shard_map/while/body/eval_jaxpr/kr,kif->rif/dot_general | solution.py:25
  89.2 8.6 %select_add_fusion.4 = f32[16,128,512]{2,0,1:T(8,128)} fusion(f32[16,128,512]{2,0,1:T(8,128)} %get-tuple-element.322, f32[16,128,512]{2,0,1:T(8,128)} %fusion.142, bf16[32,128,512]{2,1,0:T(8,128)(2,1)} %get-tuple-element.302, pred[]{:T(512)S(6)} %compare.6, s32[32]{0:T(128)S(1)} %get-tuple-element.301), kind=kOutput, calls=%fused_computation.7.clone.1 | convolution fusion | flops 70255104 | bytes 16777344 | tf_op jit(solution)/shard_map/while/body/eval_jaxpr/kr,kif->rif/dot_general | solution.py:24
  97.9 3.2 convolution_convert_fusion.8
  101.0 4.3 subtract_convert_fusion.8
  105.3 4.8 %fusion.142 = f32[16,128,512]{2,0,1:T(8,128)} fusion(bf16[32,128,512]{2,1,0:T(8,128)(2,1)S(1)} %get-tuple-element.300, s32[32]{0:T(128)S(1)} %get-tuple-element.301), kind=kOutput, calls=%fused_computation.1.clone.1 | convolution fusion | flops 67109376 | bytes 8388736 | tf_op jit(solution)/shard_map/while/body/eval_jaxpr/kr,kif->rif/dot_general | solution.py:25
  110.1 9.8 %select_add_fusion.4 = f32[16,128,512]{2,0,1:T(8,128)} fusion(f32[16,128,512]{2,0,1:T(8,128)} %get-tuple-element.322, f32[16,128,512]{2,0,1:T(8,128)} %fusion.142, bf16[32,128,512]{2,1,0:T(8,128)(2,1)} %get-tuple-element.302, pred[]{:T(512)S(6)} %compare.6, s32[32]{0:T(128)S(1)} %get-tuple-element.301), kind=kOutput, calls=%fused_computation.7.clone.1 | convolution fusion | flops 70255104 | bytes 16777344 | tf_op jit(solution)/shard_map/while/body/eval_jaxpr/kr,kif->rif/dot_general | solution.py:24
  120.0 3.3 copy.65
  123.3 2.7 convolution_convert_fusion.3
  126.0 8.7 %fusion.43 = (bf16[32,128,512]{1,2,0:T(8,128)(2,1)}, bf16[32,128,512]{1,2,0:T(8,128)(2,1)}) fusion(bf16[96,128,128]{2,1,0:T(8,128)(2,1)S(1)} %copy-done.4, bf16[32,128,512]{2,0,1:T(8,128)(2,1)S(1)} %convolution_convert_fusion.3), kind=kOutput, calls=%fused_computation.51 | convolution fusion | flops 545259520 | bytes 13631488 | tf_op jit(solution)/shard_map/while/body/eval_jaxpr/kij,kjf->kif/dot_general | solution.py:36
  134.7 8.0 %copy.71 = bf16[32,128,512]{2,0,1:T(8,128)(2,1)} copy(bf16[32,128,512]{1,2,0:T(8,128)(2,1)} %get-tuple-element.216) | data formatting | bytes 8388608 | tf_op jit(solution)/shard_map/while/body/eval_jaxpr/convert_element_type | solution.py:22
  142.7 7.9 %copy.72 = bf16[32,128,512]{2,0,1:T(8,128)(2,1)} copy(bf16[32,128,512]{1,2,0:T(8,128)(2,1)} %get-tuple-element.215) | data formatting | bytes 8388608 | tf_op jit(solution)/shard_map/while/body/eval_jaxpr/convert_element_type | solution.py:23
  150.6 3.0 fusion.86
  154.1 1.3 copy-done.7
  158.0 3.8 multiply_convert_fusion
  161.8 1.3 convolution_convert_fusion.2
  163.1 1.2 copy.74
  164.3 1.5 convolution_convert_fusion.4
  166.2 8.8 %fusion.42 = (bf16[32,128,512]{1,2,0:T(8,128)(2,1)}, bf16[32,128,512]{1,2,0:T(8,128)(2,1)}) fusion(bf16[96,128,128]{2,1,0:T(8,128)(2,1)S(1)} %copy-done.5, bf16[32,128,512]{2,0,1:T(8,128)(2,1)S(1)} %convolution_convert_fusion.4), kind=kOutput, calls=%fused_computation.48 | convolution fusion | flops 545259520 | bytes 13631488 | tf_op jit(solution)/shard_map/while/body/eval_jaxpr/kij,kif->kjf/dot_general | solution.py:58
  175.0 7.9 %copy.79 = bf16[32,128,512]{2,0,1:T(8,128)(2,1)} copy(bf16[32,128,512]{1,2,0:T(8,128)(2,1)} %get-tuple-element.214) | data formatting | bytes 8388608 | tf_op jit(solution)/shard_map/while/body/eval_jaxpr/convert_element_type | solution.py:22
  183.0 4.1 fusion.93
  187.1 7.9 %copy.80 = bf16[32,128,512]{2,0,1:T(8,128)(2,1)} copy(bf16[32,128,512]{1,2,0:T(8,128)(2,1)} %get-tuple-element.213) | data formatting | bytes 8388608 | tf_op jit(solution)/shard_map/while/body/eval_jaxpr/convert_element_type | solution.py:23
  195.0 3.5 add_convert_fusion.1
  198.6 1.3 copy.81
  199.9 4.9 %all-to-all-start.1 = ((bf16[128,8,512]{2,1,0:T(8,128)(2,1)}), bf16[128,8,512]{2,1,0:T(8,128)(2,1)}, u32[]{:S(2)}, u32[]{:S(2)}) async-start(bf16[128,8,512]{2,1,0:T(8,128)(2,1)} %bitcast.126), calls=%async_computation.1 | async-start | bytes 2097152 | tf_op jit(solution)/shard_map/all_to_all | solution.py:147
  204.8 46.0 %while.7 = (s32[]{:T(128)}, f32[20,128,512]{2,0,1:T(8,128)}, s32[2,32]{1,0:T(2,128)S(1)}, bf16[2,32,128,128]{2,3,1,0:T(8,128)(2,1)}, s32[2,32]{1,0:T(2,128)S(1)}...) while((s32[]{:T(128)}, f32[20,128,512]{2,0,1:T(8,128)}, s32[2,32]{1,0:T(2,128)S(1)}, ...), condition=%wide.region_3.4_spmd.clone, body=%wide.region_2.3_spmd.clone.sunk | while | flops 786171648 | bytes 57672704 | solution.py:68
  204.9 1.3 convolution_convert_fusion.9
  206.4 4.2 subtract_convert_fusion.9
  210.6 5.8 %fusion.150 = f32[20,128,512]{2,0,1:T(8,128)} fusion(bf16[32,128,512]{2,1,0:T(8,128)(2,1)S(1)} %get-tuple-element.310, s32[32]{0:T(128)S(1)} %get-tuple-element.311), kind=kOutput, calls=%fused_computation.25.clone.1 | convolution fusion | flops 83886720 | bytes 9437312 | tf_op jit(solution)/shard_map/while/body/eval_jaxpr/kr,kif->rif/dot_general | solution.py:25
  216.4 10.4 %select_add_fusion.5 = f32[20,128,512]{2,0,1:T(8,128)} fusion(f32[20,128,512]{2,0,1:T(8,128)} %get-tuple-element.346, f32[20,128,512]{2,0,1:T(8,128)} %fusion.150, pred[]{:T(512)S(6)} %compare.7, bf16[32,128,512]{2,1,0:T(8,128)(2,1)} %get-tuple-element.312, s32[32]{0:T(128)S(1)} %get-tuple-element.311), kind=kOutput, calls=%fused_computation.24.clone.1 | convolution fusion | flops 87818880 | bytes 19923072 | tf_op jit(solution)/shard_map/while/body/eval_jaxpr/kr,kif->rif/dot_general | solution.py:24
  226.8 1.3 convolution_convert_fusion.9
  228.4 4.2 subtract_convert_fusion.9
  232.6 5.8 %fusion.150 = f32[20,128,512]{2,0,1:T(8,128)} fusion(bf16[32,128,512]{2,1,0:T(8,128)(2,1)S(1)} %get-tuple-element.310, s32[32]{0:T(128)S(1)} %get-tuple-element.311), kind=kOutput, calls=%fused_computation.25.clone.1 | convolution fusion | flops 83886720 | bytes 9437312 | tf_op jit(solution)/shard_map/while/body/eval_jaxpr/kr,kif->rif/dot_general | solution.py:25
  238.4 12.2 %select_add_fusion.5 = f32[20,128,512]{2,0,1:T(8,128)} fusion(f32[20,128,512]{2,0,1:T(8,128)} %get-tuple-element.346, f32[20,128,512]{2,0,1:T(8,128)} %fusion.150, pred[]{:T(512)S(6)} %compare.7, bf16[32,128,512]{2,1,0:T(8,128)(2,1)} %get-tuple-element.312, s32[32]{0:T(128)S(1)} %get-tuple-element.311), kind=kOutput, calls=%fused_computation.24.clone.1 | convolution fusion | flops 87818880 | bytes 19923072 | tf_op jit(solution)/shard_map/while/body/eval_jaxpr/kr,kif->rif/dot_general | solution.py:24
  250.8 6.0 %copy.76 = f32[20,128,512]{2,1,0:T(8,128)S(1)} copy(f32[20,128,512]{2,0,1:T(8,128)} %get-tuple-element.104) | data formatting | bytes 10485760 | tf_op jit(solution)/shard_map/while | solution.py:68
  258.3 4.4 %copy.75 = f32[16,128,512]{2,1,0:T(8,128)} copy(f32[16,128,512]{2,0,1:T(8,128)S(1)} %slice.58) | data formatting | bytes 8388608 | tf_op jit(solution)/shard_map/slice | solution.py:143
  262.7 2.3 convolution_multiply_fusion
  265.0 5.7 %fusion.47 = f32[2048,512]{1,0:T(8,128)} fusion(s32[1024]{0:T(1024)S(1)} %copy-done.16, bf16[1024]{0:T(1024)(128)(2,1)S(1)} %copy-done.18, bf16[128,8,512]{2,1,0:T(8,128)(2,1)} %all-to-all-done.1), kind=kOutput, calls=%fused_computation.55 | convolution fusion | flops 2151677952 | bytes 5249024 | tf_op jit(solution)/shard_map/kr,kif->rif/dot_general | solution.py:24
  270.8 5.8 %fusion.45 = f32[2048,512]{1,0:T(8,128)} fusion(s32[1024]{0:T(1024)S(1)} %copy-done.16, bf16[1024]{0:T(1024)(128)(2,1)S(1)} %copy-done.18, bf16[128,8,512]{2,1,0:T(8,128)(2,1)} %all-to-all-done.1), kind=kOutput, calls=%fused_computation.54 | convolution fusion | flops 2153250816 | bytes 5249024 | tf_op jit(solution)/shard_map/kr,kif->rif/dot_general | solution.py:25
  276.5 140.7 %all-reduce.4.cloned.1.call-done = (f32[512,512]{1,0:T(8,128)}, f32[512,512]{1,0:T(8,128)}) async-done(((f32[512,512]{1,0:T(8,128)}, f32[512,512]{1,0:T(8,128)}), (f32[512,512]{1,0:T(8,128)}, f32[512,512]{1,0:T(8,128)})) %all-reduce.4.cloned.1.call-update) | async-done | bytes 2097168
  417.3 1.7 fusion.79
  419.5 6.6 %fusion.52 = bf16[2048,512]{1,0:T(8,128)(2,1)} fusion(f32[16,128,512]{2,1,0:T(8,128)S(1)} %copy-done.8, f32[2048,512]{1,0:T(8,128)} %fusion.47, f32[2048,512]{1,0:T(8,128)} %fusion.45, f32[2048,512]{1,0:T(8,128)S(1)} %fusion.79, s32[4]{0:T(128)S(1)} %copy-done.14, f32[512,512]{1,0:T(8,128)} %get-tuple-element.207, u32[]{:T(128)S(6)} %multiply.1), kind=kOutput, calls=%fused_computation.59 | convolution fusion | flops 13647872 | bytes 18882580 | tf_op jit(solution)/shard_map/kr,kif->rif/dot_general | solution.py:25
  (77 shorter events, 11.5 us)
Async XLA Ops:
  7.2 150.4 %copy-start = (bf16[512,512]{1,0:T(8,128)(2,1)S(1)}, bf16[512,512]{1,0:T(8,128)(2,1)}, u32[]{:S(2)}) copy-start(bf16[512,512]{1,0:T(8,128)(2,1)} %param.14) | copy-start | bytes 1572868
  8.1 0.9 copy-start.15
  9.0 0.6 copy-start.17
  14.5 12.0 %copy-start.20 = (s32[96]{0:T(128)S(1)}, s32[96]{0:T(128)}, u32[]{:S(2)}) copy-start(s32[96]{0:T(128)} %param.17) | copy-start | bytes 1156
  14.5 12.1 %copy-start.21 = (s32[96]{0:T(128)S(1)}, s32[96]{0:T(128)}, u32[]{:S(2)}) copy-start(s32[96]{0:T(128)} %param.18) | copy-start | bytes 1156
  14.5 12.2 %copy-start.9 = (bf16[2048,512]{1,0:T(8,128)(2,1)S(1)}, bf16[2048,512]{1,0:T(8,128)(2,1)}, u32[]{:S(2)}) copy-start(bf16[2048,512]{1,0:T(8,128)(2,1)} %param.13) | copy-start | bytes 6291460
  14.5 12.2 %copy-start.13 = (s32[4]{0:T(128)S(1)}, s32[4]{0:T(128)}, u32[]{:S(2)}) copy-start(s32[4]{0:T(128)} %param.19) | copy-start | bytes 52
  14.5 108.8 %all-to-all-start = ((bf16[128,8,512]{2,1,0:T(8,128)(2,1)}), bf16[128,8,512]{2,1,0:T(8,128)(2,1)}, u32[]{:S(2)}, u32[]{:S(2)}) async-start(bf16[128,8,512]{2,1,0:T(8,128)(2,1)} %fusion.69), calls=%async_computation | async-start | bytes 2097152 | tf_op jit(solution)/shard_map/all_to_all | solution.py:97
  73.8 3.2 slice-start
  123.3 2.7 copy-start.4
  150.6 3.4 copy-start.3
  150.6 4.7 %copy-start.7 = (bf16[32,128,512]{2,0,1:T(8,128)(2,1)S(1)}, bf16[32,128,512]{2,0,1:T(8,128)(2,1)}, u32[]{:S(2)}) copy-start(bf16[32,128,512]{2,0,1:T(8,128)(2,1)} %copy.72) | copy-start | bytes 12582916
  156.4 1.6 copy-start.19
  157.6 4.2 copy-start.10
  161.8 1.3 copy-start.22
  164.3 1.9 copy-start.5
  199.9 65.1 %all-to-all-start.1 = ((bf16[128,8,512]{2,1,0:T(8,128)(2,1)}), bf16[128,8,512]{2,1,0:T(8,128)(2,1)}, u32[]{:S(2)}, u32[]{:S(2)}) async-start(bf16[128,8,512]{2,1,0:T(8,128)(2,1)} %bitcast.126), calls=%async_computation.1 | async-start | bytes 2097152 | tf_op jit(solution)/shard_map/all_to_all | solution.py:147
  204.8 212.5 %all-reduce.4.cloned.1.call-start = ((), (), s32[]{:S(2)}) async-start(), calls=%async_computation.2 | async-start | bytes 4194304
  204.8 1.6 copy-start.6
  226.8 1.6 copy-start.6
  250.8 6.0 %copy-start.2 = (f32[20,128,512]{2,0,1:T(8,128)S(1)}, f32[20,128,512]{2,0,1:T(8,128)}, u32[]{:S(2)}) copy-start(f32[20,128,512]{2,0,1:T(8,128)} %get-tuple-element.104) | copy-start | bytes 15728644
  258.3 4.4 %copy-start.11 = (bf16[16,128,512]{2,1,0:T(8,128)(2,1)S(1)}, bf16[16,128,512]{2,1,0:T(8,128)(2,1)}, u32[]{:S(2)}) copy-start(bf16[16,128,512]{2,1,0:T(8,128)(2,1)} %copy-done.10) | copy-start | bytes 6291460
  258.3 4.4 %copy-start.23 = (bf16[2048,512]{1,0:T(8,128)(2,1)S(1)}, bf16[2048,512]{1,0:T(8,128)(2,1)}, u32[]{:S(2)}) copy-start(bf16[2048,512]{1,0:T(8,128)(2,1)} %copy-done.22) | copy-start | bytes 6291460
  262.7 2.3 copy-start.16
  262.7 2.3 copy-start.18
  270.8 146.5 %copy-start.14 = (s32[4]{0:T(128)S(1)}, s32[4]{0:T(128)}, u32[]{:S(2)}) copy-start(s32[4]{0:T(128)} %param.19) | copy-start | bytes 52
  417.3 2.2 copy-start.8
  419.5 6.6 %copy-start.12 = (f32[512,512]{1,0:T(8,128)S(1)}, f32[512,512]{1,0:T(8,128)}, u32[]{:S(2)}) copy-start(f32[512,512]{1,0:T(8,128)} %get-tuple-element.363) | copy-start | bytes 3145732
  419.5 7.6 %copy-start.1 = (bf16[512,512]{1,0:T(8,128)(2,1)S(1)}, bf16[512,512]{1,0:T(8,128)(2,1)}, u32[]{:S(2)}) copy-start(bf16[512,512]{1,0:T(8,128)(2,1)} %param.14) | copy-start | bytes 1572868
Sparse Core Ops, SparseCore 0:
  265.1 152.1 all-reduce.3
where the time goes:
time: 438 us; the launch traced here: 434 us
  matrix products  154 us (35%)
  waiting for transfers between devices  141 us (32%)
  local copies, waits for them, and re-layouts  61.2 us (14%)
  blocking collectives  45.4 us (10%)
  starting transfers between devices  16.9 us (4%)
  between operations  14.8 us (3%)
    unnamed x2, waiting for transfers between devices  141 us
    dot_general x8, matrix products, add_into(): jnp.einsum('kr,kif->rif', selector, upper, preferred_element_type=jnp.flo...  55.5 us
    all_gather x1, blocking collectives, per_device(): hub_all = lax.all_gather(hub_local, 'dom', axis=0, tiled=True)  45.4 us
    dot_general x8, matrix products, add_into(): jnp.einsum('kr,kif->rif', selector, lower, preferred_element_type=jnp.flo...  38.1 us
    dot_general x3, matrix products, spread_advance(): jnp.einsum('kij,kif->kjf', vals_group, picked, preferred_element_type=jnp...  17.3 us
    dot_general x3, matrix products, apply_advance(): jnp.einsum('kij,kjf->kif', vals_group, picked, preferred_element_type=jnp...  17.2 us
    convert_element_type x2, local copies, waits for them, and re-layouts, add_into(): upper = terms.astype(jnp.bfloat16)  15.9 us
    convert_element_type x2, local copies, waits for them, and re-layouts, add_into(): lower = (terms - upper.astype(jnp.float32)).astype(jnp.bfloat16)  15.9 us
  transfers between devices with their start and end apart: 3, of which 1 were waited for; matrix products, arithmetic and copies ran while one was open for 28% of the time, Pallas kernels for 0%

commit v1 on v0

--- a/solution.py
+++ b/solution.py
@@ -82,7 +82,9 @@
     hub_local = jnp.dot(hub_select, features, preferred_element_type=jnp.float32).astype(
         jnp.bfloat16
     )
-    hub_all = lax.all_gather(hub_local, "dom", axis=0, tiled=True)
+    hub_all = jnp.concatenate(
+        jax.lax.all_to_all(jnp.stack(jax.lax.axis_size("dom") * [hub_local]), "dom", 0, 0), 0
+    )
     targets = send_rows[0]
     counts = send_count[0]
     live_slots = jnp.arange(slot_count, dtype=jnp.int32)[None, :] < counts[:, None]

time: 438 us -> 419 us (0.957)
  blocking collectives: 45.4 us -> 0 us
  starting transfers between devices: 16.9 us -> 31.8 us
    all_gather x1 -> x0, blocking collectives: 45.4 us -> none  [per_device(): hub_all = lax.all_gather(hub_local, 'dom', axis=0, tiled=True)]
    all_to_all x0 -> x1, starting transfers between devices: none -> 11.5 us  [per_device(): jax.lax.all_to_all(jnp.stack(jax.lax.axis_size('dom') * [hub_local]), 'do...]
    all_to_all x1, starting transfers between devices: 4.9 us -> 10.2 us  [per_device(): lax.all_to_all(far_flat.astype(jnp.bfloat16), 'dom', split_axis=0, concat...]
    unnamed x51 -> x44, local copies, waits for them, and re-layouts: 10.9 us -> 9.63 us
  transfers between devices with their start and end apart: 3 -> 4, of which waited for: 1 -> 2; matrix products, arithmetic and copies ran while one was open for 28% -> 32% of each run, Pallas kernels for 0% -> 0%
where the time goes in v1:
time: 419 us; the launch traced here: 414 us
  matrix products  158 us (38%)
  waiting for transfers between devices  141 us (34%)
  local copies, waits for them, and re-layouts  64 us (15%)
  starting transfers between devices  31.8 us (8%)
  between operations  14.8 us (4%)
    unnamed x2, waiting for transfers between devices  141 us
    dot_general x8, matrix products, add_into(): jnp.einsum('kr,kif->rif', selector, upper, preferred_element_type=jnp.flo...  55.5 us
    dot_general x8, matrix products, add_into(): jnp.einsum('kr,kif->rif', selector, lower, preferred_element_type=jnp.flo...  38.2 us
    dot_general x3, matrix products, apply_advance(): jnp.einsum('kij,kjf->kif', vals_group, picked, preferred_element_type=jnp...  18.5 us
    dot_general x3, matrix products, spread_advance(): jnp.einsum('kij,kif->kjf', vals_group, picked, preferred_element_type=jnp...  18.5 us
    convert_element_type x2, local copies, waits for them, and re-layouts, add_into(): upper = terms.astype(jnp.bfloat16)  15.9 us
    convert_element_type x2, local copies, waits for them, and re-layouts, add_into(): lower = (terms - upper.astype(jnp.float32)).astype(jnp.bfloat16)  15.8 us
    dot_general x6, matrix products, pick_blocks(): jnp.einsum('kc,cjf->kjf', selector, blocks, preferred_element_type=jnp.fl...  13 us
  transfers between devices with their start and end apart: 4, of which 2 were waited for; matrix products, arithmetic and copies ran while one was open for 32% of the time, Pallas kernels for 0%

profile of v1, /device:TPU:1, one launch (start us, length us, event | category | flops | bytes accessed | tf_op | source)
XLA Modules:
  0.0 414.0 jit_solution(12666620024827575298)
XLA Ops:
  7.2 2.1 convolution_convert_fusion.5
  10.2 11.5 %all-to-all-start = ((bf16[128,4,512]{2,1,0:T(4,128)(2,1)}), bf16[128,4,512]{2,1,0:T(4,128)(2,1)S(1)}, u32[]{:S(2)}, u32[]{:S(2)}) async-start(bf16[128,4,512]{2,1,0:T(4,128)(2,1)} %stack.2), calls=%async_computation | async-start | bytes 1048576 | tf_op jit(solution)/shard_map/all_to_all | solution.py:86
  25.0 1.7 slice.53
  26.9 2.9 copy.65
  29.8 4.9 %fusion.69 = bf16[128,8,512]{2,1,0:T(8,128)(2,1)} fusion(bf16[2048,512]{1,0:T(8,128)(2,1)} %param.13, s32[1024]{0:T(1024)S(1)} %eq.165, bf16[1024]{0:T(1024)(128)(2,1)S(1)} %reshape.149), kind=kOutput, calls=%fused_computation.85 | convolution fusion | flops 2152202240 | bytes 3151872 | tf_op jit(solution)/shard_map/dot_general | solution.py:95
  36.1 10.1 %all-to-all-start.1 = ((bf16[128,8,512]{2,1,0:T(8,128)(2,1)}), bf16[128,8,512]{2,1,0:T(8,128)(2,1)}, u32[]{:S(2)}, u32[]{:S(2)}) async-start(bf16[128,8,512]{2,1,0:T(8,128)(2,1)} %fusion.69), calls=%async_computation.1 | async-start | bytes 2097152 | tf_op jit(solution)/shard_map/all_to_all | solution.py:99
  47.3 1.8 pad_maximum_fusion
  49.1 3.2 copy.67
  52.2 43.5 %while.6 = (s32[]{:T(128)}, f32[16,128,512]{2,0,1:T(8,128)}, s32[2,32]{1,0:T(2,128)S(1)}, bf16[2,32,128,128]{3,2,1,0:T(8,128)(2,1)S(1)}, s32[2,32]{1,0:T(2,128)S...) while((s32[]{:T(128)}, f32[16,128,512]{2,0,1:T(8,128)}, s32[2,32]{1,0:T(2,128)S(1)}, ...), condition=%wide.region_1.2_spmd.clone, body=%wide.region_0.1_spmd.clone.sunk | while | flops 768607872 | bytes 45614052 | solution.py:46
  52.3 3.2 convolution_convert_fusion.8
  55.4 4.3 %subtract_convert_fusion.8 = (bf16[32,128,512]{2,1,0:T(8,128)(2,1)S(1)}, bf16[32,128,512]{2,1,0:T(8,128)(2,1)}) fusion(bf16[32,128,512]{2,0,1:T(8,128)(2,1)S(1)} %convolution_convert_fusion.8, bf16[2,32,128,128]{3,2,1,0:T(8,128)(2,1)S(1)} %get-tuple-element.332, s32[]{:T(128)} %get-tuple-element.321), kind=kOutput, calls=%fused_computation.clone.1 | convolution fusion | flops 545259520 | bytes 13631492 | tf_op jit(solution)/shard_map/while/body/eval_jaxpr/kij,kjf->kif/dot_general | solution.py:36
  59.7 4.9 %fusion.141 = f32[16,128,512]{2,0,1:T(8,128)} fusion(bf16[32,128,512]{2,1,0:T(8,128)(2,1)S(1)} %get-tuple-element.300, s32[32]{0:T(128)S(1)} %get-tuple-element.301), kind=kOutput, calls=%fused_computation.1.clone.1 | convolution fusion | flops 67109376 | bytes 8388736 | tf_op jit(solution)/shard_map/while/body/eval_jaxpr/kr,kif->rif/dot_general | solution.py:25
  64.6 8.6 %select_add_fusion.4 = f32[16,128,512]{2,0,1:T(8,128)} fusion(f32[16,128,512]{2,0,1:T(8,128)} %get-tuple-element.322, f32[16,128,512]{2,0,1:T(8,128)} %fusion.141, bf16[32,128,512]{2,1,0:T(8,128)(2,1)} %get-tuple-element.302, pred[]{:T(512)S(6)} %compare.6, s32[32]{0:T(128)S(1)} %get-tuple-element.301), kind=kOutput, calls=%fused_computation.7.clone.1 | convolution fusion | flops 70255104 | bytes 16777344 | tf_op jit(solution)/shard_map/while/body/eval_jaxpr/kr,kif->rif/dot_general | solution.py:24
  73.2 3.2 convolution_convert_fusion.8
  76.4 4.3 %subtract_convert_fusion.8 = (bf16[32,128,512]{2,1,0:T(8,128)(2,1)S(1)}, bf16[32,128,512]{2,1,0:T(8,128)(2,1)}) fusion(bf16[32,128,512]{2,0,1:T(8,128)(2,1)S(1)} %convolution_convert_fusion.8, bf16[2,32,128,128]{3,2,1,0:T(8,128)(2,1)S(1)} %get-tuple-element.332, s32[]{:T(128)} %get-tuple-element.321), kind=kOutput, calls=%fused_computation.clone.1 | convolution fusion | flops 545259520 | bytes 13631492 | tf_op jit(solution)/shard_map/while/body/eval_jaxpr/kij,kjf->kif/dot_general | solution.py:36
  80.7 4.9 %fusion.141 = f32[16,128,512]{2,0,1:T(8,128)} fusion(bf16[32,128,512]{2,1,0:T(8,128)(2,1)S(1)} %get-tuple-element.300, s32[32]{0:T(128)S(1)} %get-tuple-element.301), kind=kOutput, calls=%fused_computation.1.clone.1 | convolution fusion | flops 67109376 | bytes 8388736 | tf_op jit(solution)/shard_map/while/body/eval_jaxpr/kr,kif->rif/dot_general | solution.py:25
  85.5 9.8 %select_add_fusion.4 = f32[16,128,512]{2,0,1:T(8,128)} fusion(f32[16,128,512]{2,0,1:T(8,128)} %get-tuple-element.322, f32[16,128,512]{2,0,1:T(8,128)} %fusion.141, bf16[32,128,512]{2,1,0:T(8,128)(2,1)} %get-tuple-element.302, pred[]{:T(512)S(6)} %compare.6, s32[32]{0:T(128)S(1)} %get-tuple-element.301), kind=kOutput, calls=%fused_computation.7.clone.1 | convolution fusion | flops 70255104 | bytes 16777344 | tf_op jit(solution)/shard_map/while/body/eval_jaxpr/kr,kif->rif/dot_general | solution.py:24
  95.7 2.5 convolution_convert_fusion.3
  98.3 10.0 %fusion.43 = (bf16[32,128,512]{1,2,0:T(8,128)(2,1)}, bf16[32,128,512]{1,2,0:T(8,128)(2,1)}) fusion(bf16[96,128,128]{2,1,0:T(8,128)(2,1)} %param.16, bf16[32,128,512]{2,0,1:T(8,128)(2,1)S(1)} %convolution_convert_fusion.3), kind=kOutput, calls=%fused_computation.51 | convolution fusion | flops 545259520 | bytes 13631488 | tf_op jit(solution)/shard_map/while/body/eval_jaxpr/kij,kjf->kif/dot_general | solution.py:36
  108.3 7.9 %copy.71 = bf16[32,128,512]{2,0,1:T(8,128)(2,1)} copy(bf16[32,128,512]{1,2,0:T(8,128)(2,1)} %get-tuple-element.216) | data formatting | bytes 8388608 | tf_op jit(solution)/shard_map/while/body/eval_jaxpr/convert_element_type | solution.py:22
  116.2 7.9 %copy.72 = bf16[32,128,512]{2,0,1:T(8,128)(2,1)} copy(bf16[32,128,512]{1,2,0:T(8,128)(2,1)} %get-tuple-element.215) | data formatting | bytes 8388608 | tf_op jit(solution)/shard_map/while/body/eval_jaxpr/convert_element_type | solution.py:23
  124.1 3.0 fusion.85
  131.5 3.8 multiply_convert_fusion
  135.3 1.3 convolution_convert_fusion.2
  137.9 1.5 convolution_convert_fusion.4
  139.4 10.1 %fusion.42 = (bf16[32,128,512]{1,2,0:T(8,128)(2,1)}, bf16[32,128,512]{1,2,0:T(8,128)(2,1)}) fusion(bf16[96,128,128]{2,1,0:T(8,128)(2,1)} %param.16, bf16[32,128,512]{2,0,1:T(8,128)(2,1)S(1)} %convolution_convert_fusion.4), kind=kOutput, calls=%fused_computation.48 | convolution fusion | flops 545259520 | bytes 13631488 | tf_op jit(solution)/shard_map/while/body/eval_jaxpr/kij,kif->kjf/dot_general | solution.py:58
  149.5 7.9 %copy.79 = bf16[32,128,512]{2,0,1:T(8,128)(2,1)} copy(bf16[32,128,512]{1,2,0:T(8,128)(2,1)} %get-tuple-element.214) | data formatting | bytes 8388608 | tf_op jit(solution)/shard_map/while/body/eval_jaxpr/convert_element_type | solution.py:22
  157.5 4.2 %fusion.92 = f32[8,128,512]{2,0,1:T(8,128)} fusion(bf16[32,128,512]{2,0,1:T(8,128)(2,1)} %copy.79, s32[32]{0:T(128)S(1)} %slice_add_fusion), kind=kOutput, calls=%fused_computation.109 | convolution fusion | flops 33554688 | bytes 6291584 | tf_op jit(solution)/shard_map/while/body/eval_jaxpr/kr,kif->rif/dot_general | solution.py:24
  161.6 7.9 %copy.80 = bf16[32,128,512]{2,0,1:T(8,128)(2,1)} copy(bf16[32,128,512]{1,2,0:T(8,128)(2,1)} %get-tuple-element.213) | data formatting | bytes 8388608 | tf_op jit(solution)/shard_map/while/body/eval_jaxpr/convert_element_type | solution.py:23
  169.5 3.5 add_convert_fusion.1
  173.0 1.3 copy.81
  174.3 10.2 %all-to-all-start.2 = ((bf16[128,8,512]{2,1,0:T(8,128)(2,1)}), bf16[128,8,512]{2,1,0:T(8,128)(2,1)}, u32[]{:S(2)}, u32[]{:S(2)}) async-start(bf16[128,8,512]{2,1,0:T(8,128)(2,1)} %bitcast.123), calls=%async_computation.2 | async-start | bytes 2097152 | tf_op jit(solution)/shard_map/all_to_all | solution.py:149
  184.6 45.9 %while.7 = (s32[]{:T(128)}, f32[20,128,512]{2,0,1:T(8,128)}, s32[2,32]{1,0:T(2,128)S(1)}, bf16[2,32,128,128]{2,3,1,0:T(8,128)(2,1)}, s32[2,32]{1,0:T(2,128)S(1)}...) while((s32[]{:T(128)}, f32[20,128,512]{2,0,1:T(8,128)}, s32[2,32]{1,0:T(2,128)S(1)}, ...), condition=%wide.region_3.4_spmd.clone, body=%wide.region_2.3_spmd.clone.sunk | while | flops 786171648 | bytes 57672704 | solution.py:68
  186.2 4.2 %subtract_convert_fusion.9 = (bf16[32,128,512]{2,1,0:T(8,128)(2,1)S(1)}, bf16[32,128,512]{2,1,0:T(8,128)(2,1)}) fusion(bf16[32,128,512]{2,0,1:T(8,128)(2,1)S(1)} %convolution_convert_fusion.9, bf16[2,32,128,128]{2,3,1,0:T(8,128)(2,1)S(1)} %copy-done.4, s32[]{:T(128)} %get-tuple-element.345), kind=kOutput, calls=%fused_computation.23.clone.1 | convolution fusion | flops 545259520 | bytes 13631492 | tf_op jit(solution)/shard_map/while/body/eval_jaxpr/kij,kif->kjf/dot_general | solution.py:58
  190.4 5.8 %fusion.149 = f32[20,128,512]{2,0,1:T(8,128)} fusion(bf16[32,128,512]{2,1,0:T(8,128)(2,1)S(1)} %get-tuple-element.310, s32[32]{0:T(128)S(1)} %get-tuple-element.311), kind=kOutput, calls=%fused_computation.25.clone.1 | convolution fusion | flops 83886720 | bytes 9437312 | tf_op jit(solution)/shard_map/while/body/eval_jaxpr/kr,kif->rif/dot_general | solution.py:25
  196.2 10.3 %select_add_fusion.5 = f32[20,128,512]{2,0,1:T(8,128)} fusion(f32[20,128,512]{2,0,1:T(8,128)} %get-tuple-element.346, f32[20,128,512]{2,0,1:T(8,128)} %fusion.149, pred[]{:T(512)S(6)} %compare.7, bf16[32,128,512]{2,1,0:T(8,128)(2,1)} %get-tuple-element.312, s32[32]{0:T(128)S(1)} %get-tuple-element.311), kind=kOutput, calls=%fused_computation.24.clone.1 | convolution fusion | flops 87818880 | bytes 19923072 | tf_op jit(solution)/shard_map/while/body/eval_jaxpr/kr,kif->rif/dot_general | solution.py:24
  206.6 1.3 convolution_convert_fusion.9
  208.1 4.2 %subtract_convert_fusion.9 = (bf16[32,128,512]{2,1,0:T(8,128)(2,1)S(1)}, bf16[32,128,512]{2,1,0:T(8,128)(2,1)}) fusion(bf16[32,128,512]{2,0,1:T(8,128)(2,1)S(1)} %convolution_convert_fusion.9, bf16[2,32,128,128]{2,3,1,0:T(8,128)(2,1)S(1)} %copy-done.4, s32[]{:T(128)} %get-tuple-element.345), kind=kOutput, calls=%fused_computation.23.clone.1 | convolution fusion | flops 545259520 | bytes 13631492 | tf_op jit(solution)/shard_map/while/body/eval_jaxpr/kij,kif->kjf/dot_general | solution.py:58
  212.4 5.8 %fusion.149 = f32[20,128,512]{2,0,1:T(8,128)} fusion(bf16[32,128,512]{2,1,0:T(8,128)(2,1)S(1)} %get-tuple-element.310, s32[32]{0:T(128)S(1)} %get-tuple-element.311), kind=kOutput, calls=%fused_computation.25.clone.1 | convolution fusion | flops 83886720 | bytes 9437312 | tf_op jit(solution)/shard_map/while/body/eval_jaxpr/kr,kif->rif/dot_general | solution.py:25
  218.1 12.1 %select_add_fusion.5 = f32[20,128,512]{2,0,1:T(8,128)} fusion(f32[20,128,512]{2,0,1:T(8,128)} %get-tuple-element.346, f32[20,128,512]{2,0,1:T(8,128)} %fusion.149, pred[]{:T(512)S(6)} %compare.7, bf16[32,128,512]{2,1,0:T(8,128)(2,1)} %get-tuple-element.312, s32[32]{0:T(128)S(1)} %get-tuple-element.311), kind=kOutput, calls=%fused_computation.24.clone.1 | convolution fusion | flops 87818880 | bytes 19923072 | tf_op jit(solution)/shard_map/while/body/eval_jaxpr/kr,kif->rif/dot_general | solution.py:24
  230.5 6.0 %copy.76 = f32[20,128,512]{2,1,0:T(8,128)S(1)} copy(f32[20,128,512]{2,0,1:T(8,128)} %get-tuple-element.104) | data formatting | bytes 10485760 | tf_op jit(solution)/shard_map/while | solution.py:68
  238.0 4.4 %copy.75 = f32[16,128,512]{2,1,0:T(8,128)} copy(f32[16,128,512]{2,0,1:T(8,128)S(1)} %slice.58) | data formatting | bytes 8388608 | tf_op jit(solution)/shard_map/slice | solution.py:145
  242.4 2.3 convolution_multiply_fusion
  244.7 5.7 %fusion.47 = f32[2048,512]{1,0:T(8,128)} fusion(s32[1024]{0:T(1024)S(1)} %copy-done.13, bf16[1024]{0:T(1024)(128)(2,1)S(1)} %copy-done.15, bf16[128,8,512]{2,1,0:T(8,128)(2,1)} %all-to-all-done.2), kind=kOutput, calls=%fused_computation.55 | convolution fusion | flops 2151677952 | bytes 5249024 | tf_op jit(solution)/shard_map/kr,kif->rif/dot_general | solution.py:24
  250.5 5.8 %fusion.45 = f32[2048,512]{1,0:T(8,128)} fusion(s32[1024]{0:T(1024)S(1)} %copy-done.13, bf16[1024]{0:T(1024)(128)(2,1)S(1)} %copy-done.15, bf16[128,8,512]{2,1,0:T(8,128)(2,1)} %all-to-all-done.2), kind=kOutput, calls=%fused_computation.54 | convolution fusion | flops 2153250816 | bytes 5249024 | tf_op jit(solution)/shard_map/kr,kif->rif/dot_general | solution.py:25
  256.2 140.7 %all-reduce.4.cloned.1.call-done = (f32[512,512]{1,0:T(8,128)}, f32[512,512]{1,0:T(8,128)}) async-done(((f32[512,512]{1,0:T(8,128)}, f32[512,512]{1,0:T(8,128)}), (f32[512,512]{1,0:T(8,128)}, f32[512,512]{1,0:T(8,128)})) %all-reduce.4.cloned.1.call-update) | async-done | bytes 2097168
  396.9 1.7 fusion.78
  399.1 6.6 %fusion.52 = bf16[2048,512]{1,0:T(8,128)(2,1)} fusion(f32[16,128,512]{2,1,0:T(8,128)S(1)} %copy-done.6, f32[2048,512]{1,0:T(8,128)} %fusion.47, f32[2048,512]{1,0:T(8,128)} %fusion.45, f32[2048,512]{1,0:T(8,128)S(1)} %fusion.78, s32[4]{0:T(128)S(1)} %copy-done.11, f32[512,512]{1,0:T(8,128)} %get-tuple-element.207, u32[]{:T(128)S(6)} %multiply.1), kind=kOutput, calls=%fused_computation.59 | convolution fusion | flops 13647872 | bytes 18882580 | tf_op jit(solution)/shard_map/kr,kif->rif/dot_general | solution.py:25
  (72 shorter events, 17.3 us)
Async XLA Ops:
  7.2 123.9 %copy-start = (bf16[512,512]{1,0:T(8,128)(2,1)S(1)}, bf16[512,512]{1,0:T(8,128)(2,1)}, u32[]{:S(2)}) copy-start(bf16[512,512]{1,0:T(8,128)(2,1)} %param.14) | copy-start | bytes 1572868
  7.2 19.6 %copy-start.18 = (s32[96]{0:T(128)S(1)}, s32[96]{0:T(128)}, u32[]{:S(2)}) copy-start(s32[96]{0:T(128)} %param.18) | copy-start | bytes 1156
  7.2 19.5 %copy-start.17 = (s32[96]{0:T(128)S(1)}, s32[96]{0:T(128)}, u32[]{:S(2)}) copy-start(s32[96]{0:T(128)} %param.17) | copy-start | bytes 1156
  10.2 25.0 %all-to-all-start = ((bf16[128,4,512]{2,1,0:T(4,128)(2,1)}), bf16[128,4,512]{2,1,0:T(4,128)(2,1)S(1)}, u32[]{:S(2)}, u32[]{:S(2)}) async-start(bf16[128,4,512]{2,1,0:T(4,128)(2,1)} %stack.2), calls=%async_computation | async-start | bytes 1048576 | tf_op jit(solution)/shard_map/all_to_all | solution.py:86
  22.6 7.1 %copy-start.12 = (s32[1024]{0:T(1024)}, s32[1024]{0:T(1024)S(1)}, u32[]{:S(2)}) copy-start(s32[1024]{0:T(1024)S(1)} %eq.165) | copy-start | bytes 12292
  23.5 6.2 %copy-start.14 = (bf16[1024]{0:T(1024)(128)(2,1)}, bf16[1024]{0:T(1024)(128)(2,1)S(1)}, u32[]{:S(2)}) copy-start(bf16[1024]{0:T(1024)(128)(2,1)S(1)} %reshape.149) | copy-start | bytes 6148
  35.3 0.8 copy-start.9
  36.1 59.7 %all-to-all-start.1 = ((bf16[128,8,512]{2,1,0:T(8,128)(2,1)}), bf16[128,8,512]{2,1,0:T(8,128)(2,1)}, u32[]{:S(2)}, u32[]{:S(2)}) async-start(bf16[128,8,512]{2,1,0:T(8,128)(2,1)} %fusion.69), calls=%async_computation.1 | async-start | bytes 2097152 | tf_op jit(solution)/shard_map/all_to_all | solution.py:99
  124.1 3.4 copy-start.3
  124.1 4.7 %copy-start.5 = (bf16[32,128,512]{2,0,1:T(8,128)(2,1)S(1)}, bf16[32,128,512]{2,0,1:T(8,128)(2,1)}, u32[]{:S(2)}) copy-start(bf16[32,128,512]{2,0,1:T(8,128)(2,1)} %copy.72) | copy-start | bytes 12582916
  129.9 1.6 copy-start.16
  131.1 4.2 %copy-start.7 = (bf16[16,128,512]{2,1,0:T(8,128)(2,1)}, bf16[16,128,512]{2,1,0:T(8,128)(2,1)S(1)}, u32[]{:S(2)}) copy-start(bf16[16,128,512]{2,1,0:T(8,128)(2,1)S(1)} %copy.73) | copy-start | bytes 6291460
  135.3 1.4 copy-start.19
  174.3 70.4 %all-to-all-start.2 = ((bf16[128,8,512]{2,1,0:T(8,128)(2,1)}), bf16[128,8,512]{2,1,0:T(8,128)(2,1)}, u32[]{:S(2)}, u32[]{:S(2)}) async-start(bf16[128,8,512]{2,1,0:T(8,128)(2,1)} %bitcast.123), calls=%async_computation.2 | async-start | bytes 2097152 | tf_op jit(solution)/shard_map/all_to_all | solution.py:149
  184.6 212.4 %all-reduce.4.cloned.1.call-start = ((), (), s32[]{:S(2)}) async-start(), calls=%async_computation.3 | async-start | bytes 4194304
  184.6 1.6 copy-start.4
  206.6 1.6 copy-start.4
  230.5 6.0 %copy-start.2 = (f32[20,128,512]{2,0,1:T(8,128)S(1)}, f32[20,128,512]{2,0,1:T(8,128)}, u32[]{:S(2)}) copy-start(f32[20,128,512]{2,0,1:T(8,128)} %get-tuple-element.104) | copy-start | bytes 15728644
  238.0 4.4 %copy-start.8 = (bf16[16,128,512]{2,1,0:T(8,128)(2,1)S(1)}, bf16[16,128,512]{2,1,0:T(8,128)(2,1)}, u32[]{:S(2)}) copy-start(bf16[16,128,512]{2,1,0:T(8,128)(2,1)} %copy-done.7) | copy-start | bytes 6291460
  238.0 4.4 %copy-start.20 = (bf16[2048,512]{1,0:T(8,128)(2,1)S(1)}, bf16[2048,512]{1,0:T(8,128)(2,1)}, u32[]{:S(2)}) copy-start(bf16[2048,512]{1,0:T(8,128)(2,1)} %copy-done.19) | copy-start | bytes 6291460
  242.4 2.3 copy-start.13
  242.4 2.3 copy-start.15
  250.5 146.5 %copy-start.11 = (s32[4]{0:T(128)S(1)}, s32[4]{0:T(128)}, u32[]{:S(2)}) copy-start(s32[4]{0:T(128)} %param.19) | copy-start | bytes 52
  396.9 2.2 copy-start.6
  399.1 6.6 %copy-start.10 = (f32[512,512]{1,0:T(8,128)S(1)}, f32[512,512]{1,0:T(8,128)}, u32[]{:S(2)}) copy-start(f32[512,512]{1,0:T(8,128)} %get-tuple-element.363) | copy-start | bytes 3145732
  399.1 7.6 %copy-start.1 = (bf16[512,512]{1,0:T(8,128)(2,1)S(1)}, bf16[512,512]{1,0:T(8,128)(2,1)}, u32[]{:S(2)}) copy-start(bf16[512,512]{1,0:T(8,128)(2,1)} %param.14) | copy-start | bytes 1572868
Sparse Core Ops, SparseCore 0:
  244.8 152.0 all-reduce.3
